TPU v7x, 32 devices: a whole 2x2x4 slice. The times are simulated.
32 devices in a mesh: fsdp: 8 (over y, x, core), tp: 4 (over z).
Axes of the slice: x: 2, y: 2, z: 4, core: 2. Of those that a mesh axis runs over, the one named last changes fastest.
Arguments:
- hidden_in: bfloat16 [4096, 2048], P(('fsdp', 'tp')), may hold values from -6 to 6
- cotangent: bfloat16 [4096, 2048], P(('fsdp', 'tp')), may hold values from -6 to 6
- seq_lengths: int32 [8, 4], P('fsdp'), may hold values from 1 to 256, 512 in all within a row
- attn_gain: bfloat16 [2048], P('fsdp'), may hold values from 0.5 to 1.5
- w_query: bfloat16 [2048, 2048], P('fsdp', 'tp'), may hold values from -0.125 to 0.125
- key_weight: bfloat16 [2048, 1024], P('fsdp', 'tp'), may hold values from -0.125 to 0.125
- value_weight: bfloat16 [2048, 1024], P('fsdp', 'tp'), may hold values from -0.125 to 0.125
- q_gain: bfloat16 [128], P('fsdp'), may hold values from 0.5 to 1.5
- k_gain: bfloat16 [128], P('fsdp'), may hold values from 0.5 to 1.5
- w_out: bfloat16 [2048, 2048], P('tp', 'fsdp'), may hold values from -0.5 to 0.5
- mlp_gain: bfloat16 [2048], P('fsdp'), may hold values from 0.5 to 1.5
- w_gate: bfloat16 [2048, 6144], P('fsdp', 'tp'), may hold values from -0.125 to 0.125
- w_up: bfloat16 [2048, 6144], P('fsdp', 'tp'), may hold values from -0.125 to 0.125
- w_down: bfloat16 [6144, 2048], P('tp', 'fsdp'), may hold values from -0.15625 to 0.15625
Outputs:
- block_out: bfloat16 [4096, 2048], P(('fsdp', 'tp'))
- grad_in: bfloat16 [4096, 2048], P(('fsdp', 'tp'))
- grad_attn_gain: float32 [2048], P('fsdp')
- grad_query: float32 [2048, 2048], P('fsdp', 'tp')
- grad_key: float32 [2048, 1024], P('fsdp', 'tp')
- grad_value: float32 [2048, 1024], P('fsdp', 'tp')
- grad_q_gain: float32 [128], P('fsdp')
- grad_k_gain: float32 [128], P('fsdp')
- grad_out_proj: float32 [2048, 2048], P('tp', 'fsdp')
- grad_mlp_gain: float32 [2048], P('fsdp')
- grad_gate: float32 [2048, 6144], P('fsdp', 'tp')
- grad_up: float32 [2048, 6144], P('fsdp', 'tp')
- grad_down: float32 [6144, 2048], P('tp', 'fsdp')
Inputs may be any that keep to these rules, and one draw needn't show every extreme that they name: `seq_lengths`: row s holds the lengths of the sequences packed, in order, in data shard s; each row sums to 512 and its largest entry is exactly 256.
All inputs are finite; a program needn't handle non-finite values.
Results may differ from a plain program's by a relative error of at most 0.025.
Values may be sent and summed in bfloat16 or wider, within the bound.
No kernel may reach another device: no remote copies, remote signals or barrier semaphores. Data moves between devices by JAX's collectives and lax.ppermute only.
A program may use at most 192 MiB of HBM per device.

v0:
```python
import math

import jax
import jax.numpy as jnp
from jax import lax
from jax.sharding import PartitionSpec as P

EPS = 1e-06
THETA = 1000000.0


def positions(lens_row, row_count):
    seq_ends = jnp.cumsum(lens_row)
    token_index = jnp.arange(row_count, dtype=jnp.int32)
    finished = token_index[:, None] >= seq_ends[None, :]
    seq_start = jnp.sum(jnp.where(finished, lens_row[None, :], 0), axis=1)
    return (token_index, seq_start)


def rope_tables(offset, head_width):
    half_width = head_width // 2
    frequency = jnp.exp(
        jnp.arange(half_width, dtype=jnp.float32) * (-2.0 * math.log(THETA) / head_width)
    )
    phase_angle = offset.astype(jnp.float32)[:, None] * frequency[None, :]
    return (jnp.cos(phase_angle)[:, None, :], jnp.sin(phase_angle)[:, None, :])


def rotate(values, cosine, sine):
    half_width = values.shape[-1] // 2
    first_half, second_half = (values[..., :half_width], values[..., half_width:])
    return jnp.concatenate(
        [first_half * cosine - second_half * sine, second_half * cosine + first_half * sine],
        axis=-1,
    )


def unrotate(values, cosine, sine):
    half_width = values.shape[-1] // 2
    first_half, second_half = (values[..., :half_width], values[..., half_width:])
    return jnp.concatenate(
        [first_half * cosine + second_half * sine, second_half * cosine - first_half * sine],
        axis=-1,
    )


def row_norm(values, gain_vec):
    inv_rms = lax.rsqrt(jnp.mean(values * values, axis=-1, keepdims=True) + EPS)
    normed = values * inv_rms
    return (normed * gain_vec.astype(jnp.float32), normed, inv_rms)


def norm_back(incoming, normed, inv_rms, gain_vec):
    scaled = incoming * gain_vec.astype(jnp.float32)
    grad_back = inv_rms * (scaled - normed * jnp.mean(scaled * normed, axis=-1, keepdims=True))
    gain_grad = jnp.sum((incoming * normed).reshape(-1, incoming.shape[-1]), axis=0)
    return (grad_back, gain_grad)


def attend(query_rot, key_rot, value, token_index, seq_start, score_scale):
    row_count, head_count, head_width = query_rot.shape
    kv_heads = key_rot.shape[1]
    groups = head_count // kv_heads
    block_rows = min(512, row_count)
    block_count = row_count // block_rows
    query_block_list = query_rot.reshape(block_count, block_rows, kv_heads, groups, head_width)

    def block_step(block_in):
        query_block, query_pos, query_start = block_in
        scores = (
            jnp.einsum("bkgd,skd->kgbs", query_block, key_rot, preferred_element_type=jnp.float32)
            * score_scale
        )
        allowed = (token_index[None, :] <= query_pos[:, None]) & (
            token_index[None, :] >= query_start[:, None]
        )
        scores = jnp.where(allowed, scores, -1e30)
        row_max = jnp.max(scores, axis=-1, keepdims=True)
        exp_scores = jnp.exp(scores - row_max)
        row_total = jnp.sum(exp_scores, axis=-1, keepdims=True)
        prob_bf = (exp_scores / row_total).astype(jnp.bfloat16)
        block_out = jnp.einsum("kgbs,skd->bkgd", prob_bf, value, preferred_element_type=jnp.float32)
        return (block_out.astype(jnp.bfloat16), (row_max + jnp.log(row_total))[..., 0])

    block_outs, log_sums = lax.map(
        block_step,
        (
            query_block_list,
            token_index.reshape(block_count, block_rows),
            seq_start.reshape(block_count, block_rows),
        ),
    )
    return (block_outs.reshape(row_count, head_count, head_width), log_sums)


def attend_back(
    query_rot, key_rot, value, attended, d_attended, log_sums, token_index, seq_start, score_scale
):
    row_count, head_count, head_width = query_rot.shape
    kv_heads = key_rot.shape[1]
    groups = head_count // kv_heads
    block_rows = min(512, row_count)
    block_count = row_count // block_rows
    shaped = (block_count, block_rows, kv_heads, groups, head_width)

    def block_step(totals, block_in):
        key_grad, value_grad = totals
        query_block, out_block, dout_block, lse_block, query_pos, query_start = block_in
        scores = (
            jnp.einsum("bkgd,skd->kgbs", query_block, key_rot, preferred_element_type=jnp.float32)
            * score_scale
        )
        allowed = (token_index[None, :] <= query_pos[:, None]) & (
            token_index[None, :] >= query_start[:, None]
        )
        probs = jnp.where(allowed, jnp.exp(scores - lse_block[..., None]), 0.0)
        prob_bf = probs.astype(jnp.bfloat16)
        value_grad = value_grad + jnp.einsum(
            "kgbs,bkgd->skd", prob_bf, dout_block, preferred_element_type=jnp.float32
        )
        d_prob = jnp.einsum("bkgd,skd->kgbs", dout_block, value, preferred_element_type=jnp.float32)
        row_delta = jnp.transpose(
            jnp.sum(dout_block.astype(jnp.float32) * out_block.astype(jnp.float32), axis=-1),
            (1, 2, 0),
        )
        d_score = (probs * (d_prob - row_delta[..., None]) * score_scale).astype(jnp.bfloat16)
        query_grad = jnp.einsum(
            "kgbs,skd->bkgd", d_score, key_rot, preferred_element_type=jnp.float32
        )
        key_grad = key_grad + jnp.einsum(
            "kgbs,bkgd->skd", d_score, query_block, preferred_element_type=jnp.float32
        )
        return ((key_grad, value_grad), query_grad)

    empty_kv = jnp.zeros((row_count, kv_heads, head_width), jnp.float32)
    block_in = (
        query_rot.reshape(shaped),
        attended.reshape(shaped),
        d_attended.reshape(shaped),
        log_sums,
        token_index.reshape(block_count, block_rows),
        seq_start.reshape(block_count, block_rows),
    )
    (key_grad, value_grad), query_grads = lax.scan(block_step, (empty_kv, empty_kv), block_in)
    return (query_grads.reshape(row_count, head_count, head_width), key_grad, value_grad)


def local(
    hidden_in,
    cotangent,
    seq_lengths,
    attn_gain,
    w_query,
    key_weight,
    value_weight,
    q_gain,
    k_gain,
    w_out,
    mlp_gain,
    w_gate,
    w_up,
    w_down,
):
    gain_attn, wq_full, wk_full, wv_full, gain_query, gain_key, wo_full = (
        lax.all_gather(attn_gain, "fsdp", axis=0, tiled=True),
        lax.all_gather(w_query, "fsdp", axis=0, tiled=True),
        lax.all_gather(key_weight, "fsdp", axis=0, tiled=True),
        lax.all_gather(value_weight, "fsdp", axis=0, tiled=True),
        lax.all_gather(q_gain, "fsdp", axis=0, tiled=True),
        lax.all_gather(k_gain, "fsdp", axis=0, tiled=True),
        lax.all_gather(w_out, "fsdp", axis=1, tiled=True),
    )
    feedforward_gain, wg_full, wu_full, wd_full = (
        lax.all_gather(mlp_gain, "fsdp", axis=0, tiled=True),
        lax.all_gather(w_gate, "fsdp", axis=0, tiled=True),
        lax.all_gather(w_up, "fsdp", axis=0, tiled=True),
        lax.all_gather(w_down, "fsdp", axis=1, tiled=True),
    )
    head_width = gain_query.shape[0]
    score_scale = 1.0 / math.sqrt(head_width)
    x_float = hidden_in.astype(jnp.float32)
    normed_in, hat_in, inv_in = row_norm(x_float, gain_attn)
    attn_in = lax.all_gather(normed_in.astype(jnp.bfloat16), "tp", axis=0, tiled=True)
    row_count = attn_in.shape[0]
    token_index, seq_start = positions(seq_lengths[0], row_count)
    cosine, sine = rope_tables(token_index - seq_start, head_width)
    query = jnp.dot(attn_in, wq_full, preferred_element_type=jnp.float32).reshape(
        row_count, -1, head_width
    )
    key_proj = jnp.dot(attn_in, wk_full, preferred_element_type=jnp.float32).reshape(
        row_count, -1, head_width
    )
    value = (
        jnp.dot(attn_in, wv_full, preferred_element_type=jnp.float32)
        .astype(jnp.bfloat16)
        .reshape(row_count, -1, head_width)
    )
    q_scaled, q_hat, q_inv = row_norm(query, gain_query)
    k_scaled, k_hat, k_inv = row_norm(key_proj, gain_key)
    query_rot = rotate(q_scaled, cosine, sine).astype(jnp.bfloat16)
    key_rot = rotate(k_scaled, cosine, sine).astype(jnp.bfloat16)
    attended, log_sums = attend(query_rot, key_rot, value, token_index, seq_start, score_scale)
    attended_flat = attended.reshape(row_count, -1)
    residual = x_float + lax.psum_scatter(
        jnp.dot(attended_flat, wo_full, preferred_element_type=jnp.float32),
        "tp",
        scatter_dimension=0,
        tiled=True,
    )
    normed_mid, hat_mid, inv_mid = row_norm(residual, feedforward_gain)
    mlp_in = lax.all_gather(normed_mid.astype(jnp.bfloat16), "tp", axis=0, tiled=True)
    gate_act = jnp.dot(mlp_in, wg_full, preferred_element_type=jnp.float32)
    up_act = jnp.dot(mlp_in, wu_full, preferred_element_type=jnp.float32)
    sigmoid_gate = 1.0 / (1.0 + jnp.exp(-gate_act))
    hidden = (gate_act * sigmoid_gate * up_act).astype(jnp.bfloat16)
    block_out = (
        residual
        + lax.psum_scatter(
            jnp.dot(hidden, wd_full, preferred_element_type=jnp.float32).astype(jnp.bfloat16),
            "tp",
            scatter_dimension=0,
            tiled=True,
        ).astype(jnp.float32)
    ).astype(jnp.bfloat16)
    grad_all = lax.all_gather(cotangent, "tp", axis=0, tiled=True)
    grad_down = jnp.dot(hidden.T, grad_all, preferred_element_type=jnp.float32)
    d_hidden = jnp.dot(grad_all, wd_full.T, preferred_element_type=jnp.float32)
    d_gate = (d_hidden * up_act * sigmoid_gate * (1.0 + gate_act * (1.0 - sigmoid_gate))).astype(
        jnp.bfloat16
    )
    d_up = (d_hidden * gate_act * sigmoid_gate).astype(jnp.bfloat16)
    grad_gate = jnp.dot(mlp_in.T, d_gate, preferred_element_type=jnp.float32)
    grad_up = jnp.dot(mlp_in.T, d_up, preferred_element_type=jnp.float32)
    d_mlp_in = lax.psum_scatter(
        (
            jnp.dot(d_gate, wg_full.T, preferred_element_type=jnp.float32)
            + jnp.dot(d_up, wu_full.T, preferred_element_type=jnp.float32)
        ).astype(jnp.bfloat16),
        "tp",
        scatter_dimension=0,
        tiled=True,
    ).astype(jnp.float32)
    d_mid, grad_gain_mlp = norm_back(d_mlp_in, hat_mid, inv_mid, feedforward_gain)
    d_residual = cotangent.astype(jnp.float32) + d_mid
    d_attn = lax.all_gather(d_residual.astype(jnp.bfloat16), "tp", axis=0, tiled=True)
    grad_out_proj = jnp.dot(attended_flat.T, d_attn, preferred_element_type=jnp.float32)
    d_attended = (
        jnp.dot(d_attn, wo_full.T, preferred_element_type=jnp.float32)
        .astype(jnp.bfloat16)
        .reshape(row_count, -1, head_width)
    )
    dq_rot, dk_rot, d_value = attend_back(
        query_rot,
        key_rot,
        value,
        attended,
        d_attended,
        log_sums,
        token_index,
        seq_start,
        score_scale,
    )
    d_query, grad_gain_query = norm_back(unrotate(dq_rot, cosine, sine), q_hat, q_inv, gain_query)
    d_key, grad_gain_key = norm_back(unrotate(dk_rot, cosine, sine), k_hat, k_inv, gain_key)
    d_query_bf = d_query.reshape(row_count, -1).astype(jnp.bfloat16)
    d_key_bf = d_key.reshape(row_count, -1).astype(jnp.bfloat16)
    d_value_bf = d_value.reshape(row_count, -1).astype(jnp.bfloat16)
    grad_query = jnp.dot(attn_in.T, d_query_bf, preferred_element_type=jnp.float32)
    grad_key = jnp.dot(attn_in.T, d_key_bf, preferred_element_type=jnp.float32)
    grad_value = jnp.dot(attn_in.T, d_value_bf, preferred_element_type=jnp.float32)
    d_attn_in = lax.psum_scatter(
        (
            jnp.dot(d_query_bf, wq_full.T, preferred_element_type=jnp.float32)
            + jnp.dot(d_key_bf, wk_full.T, preferred_element_type=jnp.float32)
            + jnp.dot(d_value_bf, wv_full.T, preferred_element_type=jnp.float32)
        ).astype(jnp.bfloat16),
        "tp",
        scatter_dimension=0,
        tiled=True,
    ).astype(jnp.float32)
    d_in_norm, grad_gain_attn = norm_back(d_attn_in, hat_in, inv_in, gain_attn)
    grad_in = (d_residual + d_in_norm).astype(jnp.bfloat16)
    every_sum = (
        lax.psum_scatter(
            grad_gain_attn.astype(jnp.bfloat16), "fsdp", scatter_dimension=0, tiled=True
        ).astype(jnp.float32),
        lax.psum_scatter(
            grad_query.astype(jnp.bfloat16), "fsdp", scatter_dimension=0, tiled=True
        ).astype(jnp.float32),
        lax.psum_scatter(
            grad_key.astype(jnp.bfloat16), "fsdp", scatter_dimension=0, tiled=True
        ).astype(jnp.float32),
        lax.psum_scatter(
            grad_value.astype(jnp.bfloat16), "fsdp", scatter_dimension=0, tiled=True
        ).astype(jnp.float32),
        lax.psum_scatter(
            grad_gain_query.astype(jnp.bfloat16), "fsdp", scatter_dimension=0, tiled=True
        ).astype(jnp.float32),
        lax.psum_scatter(
            grad_gain_key.astype(jnp.bfloat16), "fsdp", scatter_dimension=0, tiled=True
        ).astype(jnp.float32),
        lax.psum_scatter(
            grad_out_proj.astype(jnp.bfloat16), "fsdp", scatter_dimension=1, tiled=True
        ).astype(jnp.float32),
        lax.psum_scatter(
            grad_gain_mlp.astype(jnp.bfloat16), "fsdp", scatter_dimension=0, tiled=True
        ).astype(jnp.float32),
        lax.psum_scatter(
            grad_gate.astype(jnp.bfloat16), "fsdp", scatter_dimension=0, tiled=True
        ).astype(jnp.float32),
        lax.psum_scatter(
            grad_up.astype(jnp.bfloat16), "fsdp", scatter_dimension=0, tiled=True
        ).astype(jnp.float32),
        lax.psum_scatter(
            grad_down.astype(jnp.bfloat16), "fsdp", scatter_dimension=1, tiled=True
        ).astype(jnp.float32),
    )
    attn_sums = every_sum[:7]
    mlp_sums = every_sum[7:]
    gain_totals = lax.psum((attn_sums[0], attn_sums[4], attn_sums[5], mlp_sums[0]), "tp")
    return (
        block_out,
        grad_in,
        gain_totals[0],
        attn_sums[1],
        attn_sums[2],
        attn_sums[3],
        gain_totals[1],
        gain_totals[2],
        attn_sums[6],
        gain_totals[3],
        mlp_sums[1],
        mlp_sums[2],
        mlp_sums[3],
    )


def solution(mesh):
    return jax.shard_map(
        local,
        mesh=mesh,
        in_specs=(
            P(("fsdp", "tp"), None),
            P(("fsdp", "tp"), None),
            P("fsdp", None),
            P("fsdp"),
            P("fsdp", "tp"),
            P("fsdp", "tp"),
            P("fsdp", "tp"),
            P("fsdp"),
            P("fsdp"),
            P("tp", "fsdp"),
            P("fsdp"),
            P("fsdp", "tp"),
            P("fsdp", "tp"),
            P("tp", "fsdp"),
        ),
        out_specs=(
            P(("fsdp", "tp"), None),
            P(("fsdp", "tp"), None),
            P("fsdp"),
            P("fsdp", "tp"),
            P("fsdp", "tp"),
            P("fsdp", "tp"),
            P("fsdp"),
            P("fsdp"),
            P("tp", "fsdp"),
            P("fsdp"),
            P("fsdp", "tp"),
            P("fsdp", "tp"),
            P("tp", "fsdp"),
        ),
        check_vma=False,
    )
```

profile of v0, /device:TPU:0, one launch (start us, length us, event | category | flops | bytes accessed | tf_op | source)
XLA Modules:
  0.0 1075.9 jit_solution(12785175896997641999)
XLA Ops:
  8.7 10.4 all-gather
  27.8 13.5 %all-reduce.8 = (bf16[128]{0:T(256)(128)(2,1)S(1)}, bf16[128]{0:T(256)(128)(2,1)S(1)}) all-reduce(bf16[128]{0:T(256)(128)(2,1)S(1)} %dynamic-update-slice.1, bf16[128]{0:T(256)(128)(2,1)S(1)} %dynamic-update-slice), channel_id=1, replica_groups=mesh['fsdp'=8,'tp'=4] {'fsdp'}, use_global_device_ids=true, to_apply=%add.1 | all-reduce | flops 256 | bytes 1024
  42.3 41.6 %all-gather.14.cloned.1.call-done = bf16[512,2048]{1,0:T(8,128)(2,1)} async-done(((bf16[128,2048]{1,0:T(8,128)(2,1)}), bf16[512,2048]{1,0:T(8,128)(2,1)}) %all-gather.14.cloned.1.call-update) | async-done | bytes 2097168 | tf_op jit(solution)/shard_map/all_gather | solution.py:183
  88.1 20.0 %all-gather.16.cloned.1.call-done = bf16[2048,256]{1,0:T(8,128)(2,1)} async-done(((bf16[256,256]{1,0:T(8,128)(2,1)}), bf16[2048,256]{1,0:T(8,128)(2,1)}) %all-gather.16.cloned.1.call-update) | async-done | bytes 1048592 | tf_op jit(solution)/shard_map/all_gather | solution.py:168
  111.4 26.2 %all-gather.20.cloned.1.call-done = bf16[2048,512]{1,0:T(8,128)(2,1)} async-done(((bf16[256,512]{1,0:T(8,128)(2,1)}), bf16[2048,512]{1,0:T(8,128)(2,1)}) %all-gather.20.cloned.1.call-update) | async-done | bytes 2097168 | tf_op jit(solution)/shard_map/all_gather | solution.py:166
  148.4 19.1 %all-gather.22.cloned.1.call-done = bf16[512,2048]{1,0:T(8,128)(2,1)} async-done(((bf16[512,256]{1,0:T(8,128)(2,1)}), bf16[512,2048]{1,0:T(8,128)(2,1)}) %all-gather.22.cloned.1.call-update) | async-done | bytes 2097168 | tf_op jit(solution)/shard_map/all_gather | solution.py:171
  173.2 8.9 all-gather.1
  182.1 67.2 %reduce-scatter.12.cloned.1.call-done = f32[128,2048]{1,0:T(8,128)} async-done(((f32[512,2048]{1,0:T(8,128)}), f32[128,2048]{1,0:T(8,128)}) %reduce-scatter.12.cloned.1.call-update) | async-done | bytes 1048592 | tf_op jit(solution)/shard_map/reduce_scatter | solution.py:204
  254.3 42.8 %all-gather.26.cloned.1.call-done = bf16[2048,1536]{1,0:T(8,128)(2,1)} async-done(((bf16[256,1536]{1,0:T(8,128)(2,1)}), bf16[2048,1536]{1,0:T(8,128)(2,1)}) %all-gather.26.cloned.1.call-update) | async-done | bytes 6291472 | tf_op jit(solution)/shard_map/all_gather | solution.py:175
  297.1 47.8 %all-gather.24.cloned.1.call-done = bf16[512,2048]{1,0:T(8,128)(2,1)} async-done(((bf16[128,2048]{1,0:T(8,128)(2,1)}), bf16[512,2048]{1,0:T(8,128)(2,1)}) %all-gather.24.cloned.1.call-update) | async-done | bytes 2097168 | tf_op jit(solution)/shard_map/all_gather | solution.py:211
  344.9 8.5 fusion.59
  353.5 37.6 %all-gather.28.cloned.1.call-done = bf16[2048,1536]{1,0:T(8,128)(2,1)} async-done(((bf16[256,1536]{1,0:T(8,128)(2,1)}), bf16[2048,1536]{1,0:T(8,128)(2,1)}) %all-gather.28.cloned.1.call-update) | async-done | bytes 6291472 | tf_op jit(solution)/shard_map/all_gather | solution.py:176
  391.1 8.6 fusion.60
  399.6 38.5 %all-gather.32.cloned.1.call-done = bf16[512,2048]{1,0:T(8,128)(2,1)} async-done(((bf16[128,2048]{1,0:T(8,128)(2,1)}), bf16[512,2048]{1,0:T(8,128)(2,1)}) %all-gather.32.cloned.1.call-update) | async-done | bytes 2097168 | tf_op jit(solution)/shard_map/all_gather | solution.py:225
  438.2 47.3 %all-gather.30.cloned.1.call-done = bf16[1536,2048]{1,0:T(8,128)(2,1)} async-done(((bf16[1536,256]{1,0:T(8,128)(2,1)}), bf16[1536,2048]{1,0:T(8,128)(2,1)}) %all-gather.30.cloned.1.call-update) | async-done | bytes 6291472 | tf_op jit(solution)/shard_map/all_gather | solution.py:177
  485.5 11.0 %multiply_convert_fusion = (bf16[512,1536]{1,0:T(8,128)(2,1)S(1)}, bf16[512,1536]{1,0:T(8,128)(2,1)S(1)}, bf16[512,1536]{1,0:T(8,128)(2,1)}) fusion(f32[512,1536]{1,0:T(8,128)} %fusion.59, f32[512,1536]{1,0:T(8,128)} %fusion.60, bf16[512,2048]{1,0:T(8,128)(2,1)} %all-gather.32.cloned.1.call-done, bf16[1536,2048]{1,0:T(8,128)(2,1)} %all-gather.30.cloned.1.call-done), kind=kOutput, calls=%fused_computation.18 | convolution fusion | flops 3233808384 | bytes 19398656 | tf_op jit(solution)/shard_map/dot_general | solution.py:227
  496.5 6.7 fusion.61
  508.1 43.7 %reduce-scatter.16.cloned.1.call-done = bf16[128,2048]{1,0:T(8,128)(2,1)} async-done(((bf16[512,2048]{1,0:T(8,128)(2,1)}), bf16[128,2048]{1,0:T(8,128)(2,1)}) %reduce-scatter.16.cloned.1.call-update) | async-done | bytes 524304 | tf_op jit(solution)/shard_map/reduce_scatter | solution.py:234
  555.9 44.8 %all-gather.34.cloned.1.call-done = bf16[512,2048]{1,0:T(8,128)(2,1)} async-done(((bf16[128,2048]{1,0:T(8,128)(2,1)}), bf16[512,2048]{1,0:T(8,128)(2,1)}) %all-gather.34.cloned.1.call-update) | async-done | bytes 2097168 | tf_op jit(solution)/shard_map/all_gather | solution.py:245
  623.2 8.3 convolution_convert_fusion.2
  631.8 8.1 convolution_convert_fusion.1
  639.9 8.2 convolution_convert_fusion
  682.6 8.0 convolution_convert_fusion.5
  708.6 47.4 %reduce-scatter.28.cloned.1.call-done = bf16[256,1536]{1,0:T(8,128)(2,1)} async-done(((bf16[2048,1536]{1,0:T(8,128)(2,1)}), bf16[256,1536]{1,0:T(8,128)(2,1)}) %reduce-scatter.28.cloned.1.call-update) | async-done | bytes 786448 | tf_op jit(solution)/shard_map/reduce_scatter | solution.py:308
  758.4 62.6 %reduce-scatter.30.cloned.1.call-done = bf16[256,1536]{1,0:T(8,128)(2,1)} async-done(((bf16[2048,1536]{1,0:T(8,128)(2,1)}), bf16[256,1536]{1,0:T(8,128)(2,1)}) %reduce-scatter.30.cloned.1.call-update) | async-done | bytes 786448 | tf_op jit(solution)/shard_map/reduce_scatter | solution.py:311
  823.5 62.4 %reduce-scatter.32.cloned.1.call-done = bf16[1536,256]{1,0:T(8,128)(2,1)} async-done(((bf16[1536,2048]{1,0:T(8,128)(2,1)}), bf16[1536,256]{1,0:T(8,128)(2,1)}) %reduce-scatter.32.cloned.1.call-update) | async-done | bytes 786448 | tf_op jit(solution)/shard_map/reduce_scatter | solution.py:314
  888.3 42.0 %reduce-scatter.20.cloned.1.call-done = bf16[256,512]{1,0:T(8,128)(2,1)} async-done(((bf16[2048,512]{1,0:T(8,128)(2,1)}), bf16[256,512]{1,0:T(8,128)(2,1)}) %reduce-scatter.20.cloned.1.call-update) | async-done | bytes 262160 | tf_op jit(solution)/shard_map/reduce_scatter | solution.py:287
  932.1 42.5 %reduce-scatter.26.cloned.1.call-done = bf16[512,256]{1,0:T(8,128)(2,1)} async-done(((bf16[512,2048]{1,0:T(8,128)(2,1)}), bf16[512,256]{1,0:T(8,128)(2,1)}) %reduce-scatter.26.cloned.1.call-update) | async-done | bytes 262160 | tf_op jit(solution)/shard_map/reduce_scatter | solution.py:302
  976.3 44.2 %reduce-scatter.18.cloned.1.call-done = bf16[128,2048]{1,0:T(8,128)(2,1)} async-done(((bf16[512,2048]{1,0:T(8,128)(2,1)}), bf16[128,2048]{1,0:T(8,128)(2,1)}) %reduce-scatter.18.cloned.1.call-update) | async-done | bytes 524304 | tf_op jit(solution)/shard_map/reduce_scatter | solution.py:271
  1022.0 13.8 %all-reduce.7 = (bf16[2048]{0:T(1024)(128)(2,1)S(1)}, bf16[128]{0:T(256)(128)(2,1)S(1)}, bf16[128]{0:T(256)(128)(2,1)S(1)}, bf16[2048]{0:T(1024)(128)(2,1)S(1)}) all-reduce(bf16[2048]{0:T(1024)(128)(2,1)S(1)} %get-tuple-element.68, bf16[128]{0:T(256)(128)(2,1)S(1)} %fusion.40, ...), channel_id=6, replica_groups=mesh['fsdp'=8,'tp'=4] {'fsdp'}, use_global_device_ids=true, to_apply=%region_18.19.clone | all-reduce | flops 4352 | bytes 17408
  1035.9 11.8 %all-reduce.6 = (f32[256]{0:T(256)}, f32[16]{0:T(128)}, f32[16]{0:T(128)}, f32[256]{0:T(256)}) all-reduce(f32[256]{0:T(256)S(1)} %get-tuple-element.127, f32[16]{0:T(128)S(1)} %get-tuple-element.129, f32[16]{0:T(128)S(1)} %get-tuple-element.128, f32[256]{0:T(256)S(1)} %get-tuple-element.126), channel_id=1, replica_groups=mesh['fsdp'=8,'tp'=4] {'tp'}, use_global_device_ids=true, to_apply=%region_19.20 | all-reduce | flops 544 | bytes 4352 | tf_op jit(solution)/shard_map/psum | solution.py:320
  1047.7 18.2 %reduce-scatter.14.cloned.1.call-done = bf16[128,2048]{1,0:T(8,128)(2,1)} async-done(((bf16[512,2048]{1,0:T(8,128)(2,1)}), bf16[128,2048]{1,0:T(8,128)(2,1)}) %reduce-scatter.14.cloned.1.call-update) | async-done | bytes 524304 | tf_op jit(solution)/shard_map/reduce_scatter | solution.py:218
  (243 shorter events, 136.6 us)
Async XLA Ops:
  7.2 18.9 %copy-start.37 = (u32[32]{0:T(128)S(1)}, u32[32]{0:T(128)}, u32[]{:S(2)}) copy-start(u32[32]{0:T(128)} %constant.76) | copy-start | bytes 388
  7.2 20.2 %copy-start.39 = (bf16[16]{0:T(256)(128)(2,1)S(1)}, bf16[16]{0:T(256)(128)(2,1)}, u32[]{:S(2)}) copy-start(bf16[16]{0:T(256)(128)(2,1)} %param.22) | copy-start | bytes 100
  7.2 20.4 %copy-start.40 = (bf16[16]{0:T(256)(128)(2,1)S(1)}, bf16[16]{0:T(256)(128)(2,1)}, u32[]{:S(2)}) copy-start(bf16[16]{0:T(256)(128)(2,1)} %param.21) | copy-start | bytes 100
  7.2 35.1 %all-gather.18.cloned.1.call-start = ((), (), s32[]{:S(2)}) async-start(), calls=%async_computation.13 | async-start | bytes 1179648 | tf_op jit(solution)/shard_map/all_gather | solution.py:167
  7.9 76.0 %all-gather.14.cloned.1.call-start = ((), (), s32[]{:S(2)}) async-start(), calls=%async_computation.11 | async-start | bytes 2621440 | tf_op jit(solution)/shard_map/all_gather | solution.py:183
  22.4 85.7 %all-gather.16.cloned.1.call-start = ((), (), s32[]{:S(2)}) async-start(), calls=%async_computation.12 | async-start | bytes 1179648 | tf_op jit(solution)/shard_map/all_gather | solution.py:168
  23.1 114.5 %all-gather.20.cloned.1.call-start = ((), (), s32[]{:S(2)}) async-start(), calls=%async_computation.14 | async-start | bytes 2359296 | tf_op jit(solution)/shard_map/all_gather | solution.py:166
  23.7 143.8 %all-gather.22.cloned.1.call-start = ((), (), s32[]{:S(2)}) async-start(), calls=%async_computation.15 | async-start | bytes 2359296 | tf_op jit(solution)/shard_map/all_gather | solution.py:171
  24.3 225.0 %reduce-scatter.12.cloned.1.call-start = ((), (), s32[]{:S(2)}) async-start(), calls=%async_computation.16 | async-start | bytes 5242880 | tf_op jit(solution)/shard_map/reduce_scatter | solution.py:204
  86.6 24.8 %copy-start.21 = (f32[512,256]{0,1:T(8,128)}, f32[512,256]{0,1:T(8,128)S(1)}, u32[]{:S(2)}) copy-start(f32[512,256]{0,1:T(8,128)S(1)} %get-tuple-element.121) | copy-start | bytes 1572868
  86.8 24.6 %copy-start.19 = (f32[512,2,128]{2,0,1:T(8,128)}, f32[512,2,128]{2,0,1:T(8,128)S(1)}, u32[]{:S(2)}) copy-start(f32[512,2,128]{2,0,1:T(8,128)S(1)} %copy.122) | copy-start | bytes 1572868
  148.4 19.1 %copy-start.35 = (bf16[2,128,2,512]{3,1,2,0:T(8,128)(2,1)}, bf16[2,128,2,512]{3,1,2,0:T(8,128)(2,1)S(1)}, u32[]{:S(2)}) copy-start(bf16[2,128,2,512]{3,1,2,0:T(8,128)(2,1)S(1)} %fusion.16) | copy-start | bytes 1572868
  172.3 77.0 %copy-start.2 = (bf16[128,2048]{1,0:T(8,128)(2,1)S(1)}, bf16[128,2048]{1,0:T(8,128)(2,1)}, u32[]{:S(2)}) copy-start(bf16[128,2048]{1,0:T(8,128)(2,1)} %param.14) | copy-start | bytes 1572868
  172.4 124.8 %all-gather.26.cloned.1.call-start = ((), (), s32[]{:S(2)}) async-start(), calls=%async_computation.18 | async-start | bytes 7077888 | tf_op jit(solution)/shard_map/all_gather | solution.py:175
  173.1 171.8 %all-gather.24.cloned.1.call-start = ((), (), s32[]{:S(2)}) async-start(), calls=%async_computation.17 | async-start | bytes 2621440 | tf_op jit(solution)/shard_map/all_gather | solution.py:211
  251.7 139.3 %all-gather.28.cloned.1.call-start = ((), (), s32[]{:S(2)}) async-start(), calls=%async_computation.19 | async-start | bytes 7077888 | tf_op jit(solution)/shard_map/all_gather | solution.py:176
  252.5 185.7 %all-gather.32.cloned.1.call-start = ((), (), s32[]{:S(2)}) async-start(), calls=%async_computation.22 | async-start | bytes 2621440 | tf_op jit(solution)/shard_map/all_gather | solution.py:225
  253.1 232.4 %all-gather.30.cloned.1.call-start = ((), (), s32[]{:S(2)}) async-start(), calls=%async_computation.20 | async-start | bytes 7077888 | tf_op jit(solution)/shard_map/all_gather | solution.py:177
  253.8 298.0 %reduce-scatter.16.cloned.1.call-start = ((), (), s32[]{:S(2)}) async-start(), calls=%async_computation.23 | async-start | bytes 2621440 | tf_op jit(solution)/shard_map/reduce_scatter | solution.py:234
  485.5 17.8 %slice-start = ((s8[6291456]{0:T(1024)(128)(4,1)}), s8[2097152]{0:T(1024)(128)(4,1)S(1)}, s32[]{:S(2)}) async-start(s8[6291456]{0:T(1024)(128)(4,1)} %bitcast.204), calls=%async_computation.33 | async-start | bytes 4194304
  508.0 92.6 %all-gather.34.cloned.1.call-start = ((), (), s32[]{:S(2)}) async-start(), calls=%async_computation.24 | async-start | bytes 2621440 | tf_op jit(solution)/shard_map/all_gather | solution.py:245
  555.6 149.6 %reduce-scatter.22.cloned.1.call-start = ((), (), s32[]{:S(2)}) async-start(), calls=%async_computation.27 | async-start | bytes 1179648 | tf_op jit(solution)/shard_map/reduce_scatter | solution.py:290
  617.0 89.9 %reduce-scatter.24.cloned.1.call-start = ((), (), s32[]{:S(2)}) async-start(), calls=%async_computation.28 | async-start | bytes 1179648 | tf_op jit(solution)/shard_map/reduce_scatter | solution.py:293
  623.1 132.9 %reduce-scatter.28.cloned.1.call-start = ((), (), s32[]{:S(2)}) async-start(), calls=%async_computation.30 | async-start | bytes 7077888 | tf_op jit(solution)/shard_map/reduce_scatter | solution.py:308
  631.5 189.5 %reduce-scatter.30.cloned.1.call-start = ((), (), s32[]{:S(2)}) async-start(), calls=%async_computation.31 | async-start | bytes 7077888 | tf_op jit(solution)/shard_map/reduce_scatter | solution.py:311
  639.9 246.0 %reduce-scatter.32.cloned.1.call-start = ((), (), s32[]{:S(2)}) async-start(), calls=%async_computation.32 | async-start | bytes 7077888 | tf_op jit(solution)/shard_map/reduce_scatter | solution.py:314
  648.2 282.1 %reduce-scatter.20.cloned.1.call-start = ((), (), s32[]{:S(2)}) async-start(), calls=%async_computation.26 | async-start | bytes 2359296 | tf_op jit(solution)/shard_map/reduce_scatter | solution.py:287
  671.5 303.0 %reduce-scatter.26.cloned.1.call-start = ((), (), s32[]{:S(2)}) async-start(), calls=%async_computation.29 | async-start | bytes 2359296 | tf_op jit(solution)/shard_map/reduce_scatter | solution.py:302
  676.1 344.5 %reduce-scatter.18.cloned.1.call-start = ((), (), s32[]{:S(2)}) async-start(), calls=%async_computation.25 | async-start | bytes 2621440 | tf_op jit(solution)/shard_map/reduce_scatter | solution.py:271
  682.6 383.3 %reduce-scatter.14.cloned.1.call-start = ((), (), s32[]{:S(2)}) async-start(), calls=%async_computation.21 | async-start | bytes 2621440 | tf_op jit(solution)/shard_map/reduce_scatter | solution.py:218
  758.4 307.5 %copy-start.10 = (bf16[128,2048]{1,0:T(8,128)(2,1)S(1)}, bf16[128,2048]{1,0:T(8,128)(2,1)}, u32[]{:S(2)}) copy-start(bf16[128,2048]{1,0:T(8,128)(2,1)} %param.15) | copy-start | bytes 1572868
  758.4 307.5 %copy-start.18 = (bf16[128,2048]{1,0:T(8,128)(2,1)S(1)}, bf16[128,2048]{1,0:T(8,128)(2,1)}, u32[]{:S(2)}) copy-start(bf16[128,2048]{1,0:T(8,128)(2,1)} %reduce-scatter.16.cloned.1.call-done) | copy-start | bytes 1572868
  (39 other events, 124.5 us)
Sparse Core Ops, SparseCore 0:
  9.9 26.1 all-gather.17
  38.2 45.6 all-gather.13
  85.9 22.1 all-gather.15
  109.8 27.7 all-gather.19
  139.3 28.0 all-gather.21
  172.5 76.7 reduce-scatter.11
  251.2 45.8 all-gather.25
  299.2 45.6 all-gather.23
  346.8 44.1 all-gather.27
  392.5 45.6 all-gather.31
  440.0 45.3 all-gather.29
  508.2 43.5 reduce-scatter.15
  555.7 44.8 all-gather.33
  617.1 34.7 reduce-scatter.21
  655.0 35.9 reduce-scatter.23
  694.2 61.7 reduce-scatter.27
  759.2 61.7 reduce-scatter.29
  824.2 61.5 reduce-scatter.31
  889.1 41.0 reduce-scatter.19
  933.4 41.0 reduce-scatter.25
  976.8 43.6 reduce-scatter.17
  1022.8 43.0 reduce-scatter.13
where the time goes:
time: 1090 us; the launch traced here: 1080 us
  waiting for transfers between devices  801 us (73%)
  matrix products  121 us (11%)
  blocking collectives  58.3 us (5%)
  other arithmetic  46.6 us (4%)
  local copies, waits for them, and re-layouts  29.6 us (3%)
  between operations  17.6 us (2%)
    reduce_scatter x1, waiting for transfers between devices, local(): lax.psum_scatter(jnp.dot(attended_flat, wo_full, preferred_element_type=j...  67.2 us
    reduce_scatter x1, waiting for transfers between devices, local(): lax.psum_scatter(grad_up.astype(jnp.bfloat16), 'fsdp', scatter_dimension=...  62.6 us
    reduce_scatter x1, waiting for transfers between devices, local(): lax.psum_scatter(grad_down.astype(jnp.bfloat16), 'fsdp', scatter_dimensio...  62.4 us
    all_gather x1, waiting for transfers between devices, local(): lax.all_gather(normed_mid.astype(jnp.bfloat16), 'tp', axis=0, tiled=True)  47.8 us
    reduce_scatter x1, waiting for transfers between devices, local(): lax.psum_scatter(grad_gate.astype(jnp.bfloat16), 'fsdp', scatter_dimensio...  47.4 us
    all_gather x1, waiting for transfers between devices, local(): lax.all_gather(w_down, 'fsdp', axis=1, tiled=True)  47.3 us
    all_gather x1, waiting for transfers between devices, local(): lax.all_gather(d_residual.astype(jnp.bfloat16), 'tp', axis=0, tiled=True)  44.8 us
    reduce_scatter x1, waiting for transfers between devices, local(): lax.psum_scatter((jnp.dot(d_query_bf, wq_full.T, preferred_element_type=j...  44.2 us
  transfers between devices with their start and end apart: 22, of which 19 were waited for; matrix products, arithmetic and copies ran while one was open for 13% of the time, Pallas kernels for 0%

commit v1 on v0

v1 whole, which is shorter than its diff:
```python
import functools
import math

import jax
import jax.numpy as jnp
from jax import lax
from jax.sharding import PartitionSpec as P

EPS = 1e-06
THETA = 1000000.0


def positions(lens_row, token_index):
    seq_ends = jnp.cumsum(lens_row)
    finished = token_index[:, None] >= seq_ends[None, :]
    seq_start = jnp.sum(jnp.where(finished, lens_row[None, :], 0), axis=1)
    return (token_index, seq_start)


def rope_tables(offset, head_width):
    half_width = head_width // 2
    frequency = jnp.exp(
        jnp.arange(half_width, dtype=jnp.float32) * (-2.0 * math.log(THETA) / head_width)
    )
    phase_angle = offset.astype(jnp.float32)[:, None] * frequency[None, :]
    return (jnp.cos(phase_angle)[:, None, :], jnp.sin(phase_angle)[:, None, :])


def rotate(values, cosine, sine):
    half_width = values.shape[-1] // 2
    first_half, second_half = (values[..., :half_width], values[..., half_width:])
    return jnp.concatenate(
        [first_half * cosine - second_half * sine, second_half * cosine + first_half * sine],
        axis=-1,
    )


def unrotate(values, cosine, sine):
    half_width = values.shape[-1] // 2
    first_half, second_half = (values[..., :half_width], values[..., half_width:])
    return jnp.concatenate(
        [first_half * cosine + second_half * sine, second_half * cosine - first_half * sine],
        axis=-1,
    )


def row_norm(values, gain_vec):
    inv_rms = lax.rsqrt(jnp.mean(values * values, axis=-1, keepdims=True) + EPS)
    normed = values * inv_rms
    return (normed * gain_vec.astype(jnp.float32), normed, inv_rms)


def norm_back(incoming, normed, inv_rms, gain_vec):
    scaled = incoming * gain_vec.astype(jnp.float32)
    grad_back = inv_rms * (scaled - normed * jnp.mean(scaled * normed, axis=-1, keepdims=True))
    gain_grad = jnp.sum((incoming * normed).reshape(-1, incoming.shape[-1]), axis=0)
    return (grad_back, gain_grad)


def attend(query_rot, key_rot, value, token_index, seq_start, score_scale):
    row_count, head_count, head_width = query_rot.shape
    kv_heads = key_rot.shape[1]
    groups = head_count // kv_heads
    block_rows = min(512, row_count)
    block_count = row_count // block_rows
    query_block_list = query_rot.reshape(block_count, block_rows, kv_heads, groups, head_width)

    def block_step(block_in):
        query_block, query_pos, query_start = block_in
        scores = (
            jnp.einsum("bkgd,skd->kgbs", query_block, key_rot, preferred_element_type=jnp.float32)
            * score_scale
        )
        allowed = (token_index[None, :] <= query_pos[:, None]) & (
            token_index[None, :] >= query_start[:, None]
        )
        scores = jnp.where(allowed, scores, -1e30)
        row_max = jnp.max(scores, axis=-1, keepdims=True)
        exp_scores = jnp.exp(scores - row_max)
        row_total = jnp.sum(exp_scores, axis=-1, keepdims=True)
        prob_bf = (exp_scores / row_total).astype(jnp.bfloat16)
        block_out = jnp.einsum("kgbs,skd->bkgd", prob_bf, value, preferred_element_type=jnp.float32)
        return (block_out.astype(jnp.bfloat16), (row_max + jnp.log(row_total))[..., 0])

    block_outs, log_sums = lax.map(
        block_step,
        (
            query_block_list,
            token_index.reshape(block_count, block_rows),
            seq_start.reshape(block_count, block_rows),
        ),
    )
    return (block_outs.reshape(row_count, head_count, head_width), log_sums)


def attend_back(
    query_rot, key_rot, value, attended, d_attended, log_sums, token_index, seq_start, score_scale
):
    row_count, head_count, head_width = query_rot.shape
    kv_heads = key_rot.shape[1]
    groups = head_count // kv_heads
    block_rows = min(512, row_count)
    block_count = row_count // block_rows
    shaped = (block_count, block_rows, kv_heads, groups, head_width)

    def block_step(totals, block_in):
        key_grad, value_grad = totals
        query_block, out_block, dout_block, lse_block, query_pos, query_start = block_in
        scores = (
            jnp.einsum("bkgd,skd->kgbs", query_block, key_rot, preferred_element_type=jnp.float32)
            * score_scale
        )
        allowed = (token_index[None, :] <= query_pos[:, None]) & (
            token_index[None, :] >= query_start[:, None]
        )
        probs = jnp.where(allowed, jnp.exp(scores - lse_block[..., None]), 0.0)
        prob_bf = probs.astype(jnp.bfloat16)
        value_grad = value_grad + jnp.einsum(
            "kgbs,bkgd->skd", prob_bf, dout_block, preferred_element_type=jnp.float32
        )
        d_prob = jnp.einsum("bkgd,skd->kgbs", dout_block, value, preferred_element_type=jnp.float32)
        row_delta = jnp.transpose(
            jnp.sum(dout_block.astype(jnp.float32) * out_block.astype(jnp.float32), axis=-1),
            (1, 2, 0),
        )
        d_score = (probs * (d_prob - row_delta[..., None]) * score_scale).astype(jnp.bfloat16)
        query_grad = jnp.einsum(
            "kgbs,skd->bkgd", d_score, key_rot, preferred_element_type=jnp.float32
        )
        key_grad = key_grad + jnp.einsum(
            "kgbs,bkgd->skd", d_score, query_block, preferred_element_type=jnp.float32
        )
        return ((key_grad, value_grad), query_grad)

    empty_kv = jnp.zeros((row_count, kv_heads, head_width), jnp.float32)
    block_in = (
        query_rot.reshape(shaped),
        attended.reshape(shaped),
        d_attended.reshape(shaped),
        log_sums,
        token_index.reshape(block_count, block_rows),
        seq_start.reshape(block_count, block_rows),
    )
    (key_grad, value_grad), query_grads = lax.scan(block_step, (empty_kv, empty_kv), block_in)
    return (query_grads.reshape(row_count, head_count, head_width), key_grad, value_grad)


def local(
    fsdp_size,
    tp_size,
    hidden_in,
    cotangent,
    seq_lengths,
    attn_gain,
    w_query,
    key_weight,
    value_weight,
    q_gain,
    k_gain,
    w_out,
    mlp_gain,
    w_gate,
    w_up,
    w_down,
):
    bf, f32 = jnp.bfloat16, jnp.float32
    core = lax.axis_index("fsdp") % 2
    place = lax.axis_index("tp")
    same_core = [[i for i in range(fsdp_size) if i % 2 == c] for c in range(2)]

    def swap(x):
        return lax.ppermute(x, "fsdp", [(i, i ^ 1) for i in range(fsdp_size)])

    def shift(x, by):
        return lax.ppermute(x, "tp", [(i, (i + by) % tp_size) for i in range(tp_size)])

    def gather_rows(x):
        pieces = [x]
        for _ in range(tp_size - 1):
            pieces.append(shift(pieces[-1], 1))
        return jnp.concatenate(pieces, axis=0)

    def scatter_rows(x):
        rows = x.shape[0] // tp_size
        total = x[:rows].astype(f32)
        got = [shift(x[s * rows : (s + 1) * rows], -s) for s in range(1, tp_size)]
        for piece in got:
            total = total + piece.astype(f32)
        return total

    def dot(a, b):
        return jnp.dot(a, b, preferred_element_type=f32)

    def dot_tn(a, b):
        return lax.dot_general(a, b, (((0,), (0,)), ((), ())), preferred_element_type=f32)

    def dot_nt(a, b):
        return lax.dot_general(a, b, (((1,), (1,)), ((), ())), preferred_element_type=f32)

    sizes = [attn_gain.shape[0], mlp_gain.shape[0], q_gain.shape[0], k_gain.shape[0]]
    gains = lax.all_gather(
        jnp.concatenate([attn_gain, mlp_gain, q_gain, k_gain])[None], "fsdp", axis=0, tiled=True
    )
    cuts = [sum(sizes[:i]) for i in range(5)]
    gain_attn, feedforward_gain, gain_query, gain_key = (
        gains[:, cuts[i] : cuts[i + 1]].reshape(-1) for i in range(4)
    )
    head_width = gain_query.shape[0]
    score_scale = 1.0 / math.sqrt(head_width)

    q_cols, k_cols, v_cols = w_query.shape[1], key_weight.shape[1], value_weight.shape[1]
    wqkv = lax.all_gather(
        jnp.concatenate([w_query, key_weight, value_weight], axis=1), "fsdp", axis=0, tiled=True
    )
    wo_full = lax.all_gather(w_out, "fsdp", axis=1, tiled=True)
    half = w_gate.shape[1] // 2

    def mine(w, axis):
        return lax.dynamic_slice_in_dim(w, core * half, half, axis)

    def theirs(w, axis):
        return lax.dynamic_slice_in_dim(w, (1 - core) * half, half, axis)

    def chip_rows(w, axis):
        own, other = mine(w, 1 - axis), swap(theirs(w, 1 - axis))
        return jnp.where(
            core == 0,
            jnp.concatenate([own, other], axis=axis),
            jnp.concatenate([other, own], axis=axis),
        )

    def gather_chips(w, axis):
        return lax.all_gather(
            w, "fsdp", axis=axis, tiled=True, axis_index_groups=same_core
        )

    wg_half = gather_chips(chip_rows(w_gate, 0), 0)
    wu_half = gather_chips(chip_rows(w_up, 0), 0)
    wd_half = gather_chips(chip_rows(w_down, 1), 1)

    x_all = gather_rows(hidden_in)
    normed_in, _, _ = row_norm(x_all.astype(f32), gain_attn)
    attn_in = normed_in.astype(bf)
    row_count = attn_in.shape[0]
    piece_rows = row_count // tp_size
    token_index = jnp.concatenate(
        [((place - s) % tp_size) * piece_rows + jnp.arange(piece_rows, dtype=jnp.int32) for s in range(tp_size)]
    )
    token_index, seq_start = positions(seq_lengths[0], token_index)
    cosine, sine = rope_tables(token_index - seq_start, head_width)
    qkv = dot(attn_in, wqkv)
    query = qkv[:, :q_cols].reshape(row_count, -1, head_width)
    key_proj = qkv[:, q_cols : q_cols + k_cols].reshape(row_count, -1, head_width)
    value = qkv[:, q_cols + k_cols :].astype(bf).reshape(row_count, -1, head_width)
    q_scaled, q_hat, q_inv = row_norm(query, gain_query)
    k_scaled, k_hat, k_inv = row_norm(key_proj, gain_key)
    query_rot = rotate(q_scaled, cosine, sine).astype(bf)
    key_rot = rotate(k_scaled, cosine, sine).astype(bf)
    attended, log_sums = attend(query_rot, key_rot, value, token_index, seq_start, score_scale)
    attended_flat = attended.reshape(row_count, -1)
    x_float = hidden_in.astype(f32)
    residual = x_float + scatter_rows(dot(attended_flat, wo_full).astype(bf))
    normed_mid, hat_mid, inv_mid = row_norm(residual, feedforward_gain)

    def both(x):
        return jnp.concatenate([x, swap(x)], axis=0)

    def from_both(x):
        own, other = x[:row_count], swap(x[row_count:])
        return (own.astype(f32) + other.astype(f32)).astype(bf)

    grad_all = both(gather_rows(cotangent))
    mlp_in = both(gather_rows(normed_mid.astype(bf)))
    gate_act = dot(mlp_in, wg_half)
    up_act = dot(mlp_in, wu_half)
    sigmoid_gate = 1.0 / (1.0 + jnp.exp(-gate_act))
    hidden = (gate_act * sigmoid_gate * up_act).astype(bf)
    d_hidden = dot_nt(grad_all, wd_half)
    d_gate = (d_hidden * up_act * sigmoid_gate * (1.0 + gate_act * (1.0 - sigmoid_gate))).astype(bf)
    d_up = (d_hidden * gate_act * sigmoid_gate).astype(bf)
    d_mlp_in = scatter_rows(
        from_both((dot_nt(d_gate, wg_half) + dot_nt(d_up, wu_half)).astype(bf))
    )
    block_out = (residual + scatter_rows(from_both(dot(hidden, wd_half).astype(bf)))).astype(bf)
    grad_down = dot_tn(hidden, grad_all)
    grad_gate = dot_tn(mlp_in, d_gate)
    grad_up = dot_tn(mlp_in, d_up)

    d_mid, grad_gain_mlp = norm_back(d_mlp_in, hat_mid, inv_mid, feedforward_gain)
    d_residual = cotangent.astype(f32) + d_mid
    d_attn = gather_rows(d_residual.astype(bf))
    grad_out_proj = dot_tn(attended_flat, d_attn)
    d_attended = dot_nt(d_attn, wo_full).astype(bf).reshape(row_count, -1, head_width)
    dq_rot, dk_rot, d_value = attend_back(
        query_rot, key_rot, value, attended, d_attended, log_sums, token_index, seq_start, score_scale,
    )
    d_query, grad_gain_query = norm_back(unrotate(dq_rot, cosine, sine), q_hat, q_inv, gain_query)
    d_key, grad_gain_key = norm_back(unrotate(dk_rot, cosine, sine), k_hat, k_inv, gain_key)
    d_qkv = jnp.concatenate(
        [g.reshape(row_count, -1).astype(bf) for g in (d_query, d_key, d_value)], axis=1
    )
    grad_qkv = dot_tn(attn_in, d_qkv)
    d_attn_in = scatter_rows(dot_nt(d_qkv, wqkv).astype(bf))
    x_own, hat_in, inv_in = row_norm(x_float, gain_attn)
    d_in_norm, grad_gain_attn = norm_back(d_attn_in, hat_in, inv_in, gain_attn)
    grad_in = (d_residual + d_in_norm).astype(bf)

    def scatter_chips(g, axis):
        part = lax.psum_scatter(
            g.astype(bf), "fsdp", scatter_dimension=axis, tiled=True, axis_index_groups=same_core
        )
        n = part.shape[axis] // 2
        own = lax.dynamic_slice_in_dim(part, core * n, n, axis)
        other = swap(lax.dynamic_slice_in_dim(part, (1 - core) * n, n, axis))
        return jnp.where(
            core == 0,
            jnp.concatenate([own, other], axis=1 - axis),
            jnp.concatenate([other, own], axis=1 - axis),
        ).astype(f32)

    out_down = scatter_chips(grad_down, 1)
    out_gate = scatter_chips(grad_gate, 0)
    out_up = scatter_chips(grad_up, 0)
    out_proj = lax.psum_scatter(
        grad_out_proj.astype(bf), "fsdp", scatter_dimension=1, tiled=True
    ).astype(f32)
    out_qkv = lax.psum_scatter(
        grad_qkv.astype(bf), "fsdp", scatter_dimension=0, tiled=True
    ).astype(f32)
    gain_grads = lax.psum(
        jnp.concatenate([grad_gain_attn, grad_gain_mlp, grad_gain_query, grad_gain_key]), ("fsdp", "tp")
    )
    where = lax.axis_index("fsdp")
    totals = [sum(sizes[:i]) * fsdp_size for i in range(4)]
    gain_out = [
        lax.dynamic_slice_in_dim(gain_grads, totals[i] + where * sizes[i], sizes[i], 0) for i in range(4)
    ]
    return (
        block_out,
        grad_in,
        gain_out[0],
        out_qkv[:, :q_cols],
        out_qkv[:, q_cols : q_cols + k_cols],
        out_qkv[:, q_cols + k_cols :],
        gain_out[2],
        gain_out[3],
        out_proj,
        gain_out[1],
        out_gate,
        out_up,
        out_down,
    )


def solution(mesh):
    return jax.shard_map(
        functools.partial(local, mesh.shape["fsdp"], mesh.shape["tp"]),
        mesh=mesh,
        in_specs=(
            P(("fsdp", "tp"), None),
            P(("fsdp", "tp"), None),
            P("fsdp", None),
            P("fsdp"),
            P("fsdp", "tp"),
            P("fsdp", "tp"),
            P("fsdp", "tp"),
            P("fsdp"),
            P("fsdp"),
            P("tp", "fsdp"),
            P("fsdp"),
            P("fsdp", "tp"),
            P("fsdp", "tp"),
            P("tp", "fsdp"),
        ),
        out_specs=(
            P(("fsdp", "tp"), None),
            P(("fsdp", "tp"), None),
            P("fsdp"),
            P("fsdp", "tp"),
            P("fsdp", "tp"),
            P("fsdp", "tp"),
            P("fsdp"),
            P("fsdp"),
            P("tp", "fsdp"),
            P("fsdp"),
            P("fsdp", "tp"),
            P("fsdp", "tp"),
            P("tp", "fsdp"),
        ),
        check_vma=False,
    )
```

time: 1090 us -> 596 us (0.55)
  waiting for transfers between devices: 801 us -> 257 us
  local copies, waits for them, and re-layouts: 29.6 us -> 65.8 us
  starting transfers between devices: 1.99 us -> 25.7 us
  matrix products: 121 us -> 102 us
  blocking collectives: 58.3 us -> 75.2 us
    reduce_scatter x11 -> x5, waiting for transfers between devices: 430 us -> 0.01 us  [the longest x3 0.01 us: scatter_chips(): lax.psum_scatter(g.astype(bf), 'fsdp', scatter_dimension=axis, tiled=True...]
    all_gather x11 -> x5, waiting for transfers between devices: 366 us -> 0.05 us  [the longest x1 0.02 us: local(): lax.all_gather(jnp.concatenate([w_query, key_weight, value_weight], axis=...]
    ppermute x0 -> x34, waiting for transfers between devices: none -> 256 us  [the longest x24 254 us: shift(): lax.ppermute(x, 'tp', [(i, (i + by) % tp_size) for i in range(tp_size)])]
    psum x1, blocking collectives: 11.8 us -> 48.7 us  [local(): lax.psum(jnp.concatenate([grad_gain_attn, grad_gain_mlp, grad_gain_query,...]
    ppermute x0 -> x34, starting transfers between devices: none -> 24.8 us  [the longest x24 21.9 us: shift(): lax.ppermute(x, 'tp', [(i, (i + by) % tp_size) for i in range(tp_size)])]
    dot_general x21 -> x15, matrix products: 110 us -> 89.1 us  [the longest x5 31.7 us: dot_tn(): lax.dot_general(a, b, (((0,), (0,)), ((), ())), preferred_element_type=f32)]
    all_gather x2 -> x0, blocking collectives: 19.3 us -> none  [the longest x1 10.4 us: local(): lax.all_gather(attn_gain, 'fsdp', axis=0, tiled=True)]
    unnamed x107 -> x181, local copies, waits for them, and re-layouts: 12 us -> 30.9 us
  transfers between devices with their start and end apart: 22 -> 44, of which waited for: 19 -> 17; matrix products, arithmetic and copies ran while one was open for 13% -> 31% of each run, Pallas kernels for 0% -> 0%
where the time goes in v1:
time: 596 us; the launch traced here: 592 us
  waiting for transfers between devices  257 us (43%)
  matrix products  102 us (17%)
  blocking collectives  75.2 us (13%)
  local copies, waits for them, and re-layouts  65.8 us (11%)
  other arithmetic  50.1 us (8%)
  starting transfers between devices  25.7 us (4%)
  between operations  16.4 us (3%)
    ppermute x24, waiting for transfers between devices, shift(): lax.ppermute(x, 'tp', [(i, (i + by) % tp_size) for i in range(tp_size)])  254 us
    psum x1, blocking collectives, local(): lax.psum(jnp.concatenate([grad_gain_attn, grad_gain_mlp, grad_gain_query,...  48.7 us
    dot_general x5, matrix products, dot_tn(): lax.dot_general(a, b, (((0,), (0,)), ((), ())), preferred_element_type=f32)  31.7 us
    unnamed x181, local copies, waits for them, and re-layouts  30.9 us
    dot_general x5, matrix products, dot(): return jnp.dot(a, b, preferred_element_type=f32)  30.8 us
    dot_general x5, matrix products, dot_nt(): lax.dot_general(a, b, (((1,), (1,)), ((), ())), preferred_element_type=f32)  26.6 us
    unnamed x1, blocking collectives  26.4 us
    ppermute x24, starting transfers between devices, shift(): lax.ppermute(x, 'tp', [(i, (i + by) % tp_size) for i in range(tp_size)])  21.9 us
  transfers between devices with their start and end apart: 44, of which 17 were waited for; matrix products, arithmetic and copies ran while one was open for 31% of the time, Pallas kernels for 0%

profile of v1, /device:TPU:0, one launch (start us, length us, event | category | flops | bytes accessed | tf_op | source)
XLA Modules:
  0.0 591.7 jit_solution(12438605041286826986)
XLA Ops:
  22.8 26.4 %all-reduce = bf16[4352]{0:T(1024)(128)(2,1)S(1)} all-reduce(bf16[4352]{0:T(1024)(128)(2,1)S(1)} %dynamic-update-slice), channel_id=2, replica_groups=mesh['fsdp'=8,'tp'=4] {'fsdp'}, use_global_device_ids=true, to_apply=%add | all-reduce | flops 4352 | bytes 17408
  51.1 10.9 %collective-permute-done.1 = bf16[128,2048]{1,0:T(8,128)(2,1)S(1)} collective-permute-done((bf16[128,2048]{1,0:T(8,128)(2,1)S(1)}, bf16[128,2048]{1,0:T(8,128)(2,1)S(1)}, u32[]{:S(2)}, u32[]{:S(2)}) %collective-permute-start.1) | collective-permute-done | bytes 524320 | tf_op jit(solution)/shard_map/ppermute | solution.py:175
  66.5 12.2 %collective-permute-done.2 = bf16[128,2048]{1,0:T(8,128)(2,1)} collective-permute-done((bf16[128,2048]{1,0:T(8,128)(2,1)S(1)}, bf16[128,2048]{1,0:T(8,128)(2,1)}, u32[]{:S(2)}, u32[]{:S(2)}) %collective-permute-start.2) | collective-permute-done | bytes 524320 | tf_op jit(solution)/shard_map/ppermute | solution.py:175
  80.3 4.7 fusion.40
  108.8 15.6 %collective-permute-done.3 = bf16[128,2048]{1,0:T(8,128)(2,1)S(1)} collective-permute-done((bf16[128,2048]{1,0:T(8,128)(2,1)S(1)}, bf16[128,2048]{1,0:T(8,128)(2,1)S(1)}, u32[]{:S(2)}, u32[]{:S(2)}) %collective-permute-start.3) | collective-permute-done | bytes 524320 | tf_op jit(solution)/shard_map/ppermute | solution.py:175
  124.5 28.3 %collective-permute-done.4 = bf16[128,2048]{1,0:T(8,128)(2,1)S(1)} collective-permute-done((bf16[128,2048]{1,0:T(8,128)(2,1)S(1)}, bf16[128,2048]{1,0:T(8,128)(2,1)S(1)}, u32[]{:S(2)}, u32[]{:S(2)}) %collective-permute-start.4) | collective-permute-done | bytes 524320 | tf_op jit(solution)/shard_map/ppermute | solution.py:175
  158.5 9.0 %collective-permute-done.6 = bf16[128,2048]{1,0:T(8,128)(2,1)} collective-permute-done((bf16[128,2048]{1,0:T(8,128)(2,1)S(1)}, bf16[128,2048]{1,0:T(8,128)(2,1)}, u32[]{:S(2)}, u32[]{:S(2)}) %collective-permute-start.6) | collective-permute-done | bytes 524320 | tf_op jit(solution)/shard_map/ppermute | solution.py:175
  168.7 12.0 %collective-permute-done.7 = bf16[128,2048]{1,0:T(8,128)(2,1)} collective-permute-done((bf16[128,2048]{1,0:T(8,128)(2,1)}, bf16[128,2048]{1,0:T(8,128)(2,1)}, u32[]{:S(2)}, u32[]{:S(2)}) %collective-permute-start.7) | collective-permute-done | bytes 524320 | tf_op jit(solution)/shard_map/ppermute | solution.py:175
  184.6 7.4 %collective-permute-done.8 = bf16[128,2048]{1,0:T(8,128)(2,1)S(1)} collective-permute-done((bf16[128,2048]{1,0:T(8,128)(2,1)}, bf16[128,2048]{1,0:T(8,128)(2,1)S(1)}, u32[]{:S(2)}, u32[]{:S(2)}) %collective-permute-start.8) | collective-permute-done | bytes 524320 | tf_op jit(solution)/shard_map/ppermute | solution.py:175
  201.0 8.8 %fusion.74 = f32[1024,768]{1,0:T(8,128)} fusion(bf16[1024,2048]{1,0:T(8,128)(2,1)} %constant_dynamic-update-slice_fusion.5, bf16[768,2048]{1,0:T(8,128)(2,1)} %all-gather.15.cloned.1.call-done), kind=kOutput, calls=%fused_computation.194 | convolution fusion | flops 3221225472 | bytes 10485760 | tf_op jit(solution)/shard_map/dot_general | solution.py:198
  217.6 8.3 %fusion.73 = f32[1024,768]{1,0:T(8,128)} fusion(bf16[1024,2048]{1,0:T(8,128)(2,1)} %constant_dynamic-update-slice_fusion, bf16[2048,768]{1,0:T(8,128)(2,1)} %all-gather.13.cloned.1.call-done), kind=kOutput, calls=%fused_computation.193 | convolution fusion | flops 3221225472 | bytes 10485760 | tf_op jit(solution)/shard_map/dot_general | solution.py:192
  226.0 11.1 %multiply_convert_fusion.1 = (bf16[1024,768]{1,0:T(8,128)(2,1)}, bf16[1024,768]{1,0:T(8,128)(2,1)S(1)}, bf16[1024,768]{1,0:T(8,128)(2,1)}) fusion(f32[1024,768]{1,0:T(8,128)} %fusion.74, f32[1024,768]{1,0:T(8,128)} %fusion.73, bf16[1024,2048]{1,0:T(8,128)(2,1)} %constant_dynamic-update-slice_fusion, bf16[2048,768]{1,0:T(8,128)(2,1)} %all-gather.11.cloned.1.call-done), kind=kOutput, calls=%fused_computation.27 | convolution fusion | flops 3233808384 | bytes 18350080 | tf_op jit(solution)/shard_map/dot_general | solution.py:192
  238.2 7.2 %convolution_convert_fusion.2 = bf16[768,2048]{1,0:T(8,128)(2,1)} fusion(bf16[1024,768]{1,0:T(8,128)(2,1)S(1)} %get-tuple-element.92, bf16[1024,2048]{1,0:T(8,128)(2,1)} %constant_dynamic-update-slice_fusion.5), kind=kOutput, calls=%fused_computation.21 | convolution fusion | flops 3222798336 | bytes 8912896 | tf_op jit(solution)/shard_map/dot_general | solution.py:195
  245.6 7.8 %convolution_convert_fusion.3 = bf16[2048,768]{1,0:T(8,128)(2,1)} fusion(bf16[1024,2048]{1,0:T(8,128)(2,1)} %constant_dynamic-update-slice_fusion, bf16[1024,768]{1,0:T(8,128)(2,1)} %get-tuple-element.93), kind=kOutput, calls=%fused_computation.22 | convolution fusion | flops 3222798336 | bytes 8912896 | tf_op jit(solution)/shard_map/dot_general | solution.py:195
  253.5 6.0 %fusion.75 = f32[1024,2048]{1,0:T(8,128)S(1)} fusion(bf16[1024,768]{1,0:T(8,128)(2,1)} %get-tuple-element.93, bf16[2048,768]{1,0:T(8,128)(2,1)} %all-gather.13.cloned.1.call-done), kind=kOutput, calls=%fused_computation.195 | convolution fusion | flops 3221225472 | bytes 13107200 | tf_op jit(solution)/shard_map/dot_general | solution.py:198
  259.5 3.7 add_convert_fusion
  267.4 3.6 convolution_convert_fusion.1
  275.1 7.5 %convolution_convert_fusion.4 = bf16[2048,768]{1,0:T(8,128)(2,1)} fusion(bf16[1024,2048]{1,0:T(8,128)(2,1)} %constant_dynamic-update-slice_fusion, bf16[1024,768]{1,0:T(8,128)(2,1)S(1)} %copy-done.82), kind=kOutput, calls=%fused_computation.23 | convolution fusion | flops 3222798336 | bytes 8912896 | tf_op jit(solution)/shard_map/dot_general | solution.py:195
  293.8 8.1 %collective-permute-done.22 = bf16[128,2048]{1,0:T(8,128)(2,1)S(1)} collective-permute-done((bf16[128,2048]{1,0:T(8,128)(2,1)S(1)}, bf16[128,2048]{1,0:T(8,128)(2,1)S(1)}, u32[]{:S(2)}, u32[]{:S(2)}) %collective-permute-start.22) | collective-permute-done | bytes 524320 | tf_op jit(solution)/shard_map/ppermute | solution.py:175
  302.1 30.1 %collective-permute-done.23 = bf16[128,2048]{1,0:T(8,128)(2,1)S(1)} collective-permute-done((bf16[128,2048]{1,0:T(8,128)(2,1)S(1)}, bf16[128,2048]{1,0:T(8,128)(2,1)S(1)}, u32[]{:S(2)}, u32[]{:S(2)}) %collective-permute-start.23) | collective-permute-done | bytes 524320 | tf_op jit(solution)/shard_map/ppermute | solution.py:175
  333.8 41.8 %collective-permute-done.15 = bf16[128,2048]{1,0:T(8,128)(2,1)S(1)} collective-permute-done((bf16[128,2048]{1,0:T(8,128)(2,1)S(1)}, bf16[128,2048]{1,0:T(8,128)(2,1)S(1)}, u32[]{:S(2)}, u32[]{:S(2)}) %collective-permute-start.15) | collective-permute-done | bytes 524320 | tf_op jit(solution)/shard_map/ppermute | solution.py:175
  381.1 12.3 %collective-permute-done.25 = bf16[128,2048]{1,0:T(8,128)(2,1)S(1)} collective-permute-done((bf16[128,2048]{1,0:T(8,128)(2,1)S(1)}, bf16[128,2048]{1,0:T(8,128)(2,1)S(1)}, u32[]{:S(2)}, u32[]{:S(2)}) %collective-permute-start.25) | collective-permute-done | bytes 524320 | tf_op jit(solution)/shard_map/ppermute | solution.py:175
  395.0 13.2 %collective-permute-done.26 = bf16[128,2048]{1,0:T(8,128)(2,1)S(1)} collective-permute-done((bf16[128,2048]{1,0:T(8,128)(2,1)S(1)}, bf16[128,2048]{1,0:T(8,128)(2,1)S(1)}, u32[]{:S(2)}, u32[]{:S(2)}) %collective-permute-start.26) | collective-permute-done | bytes 524320 | tf_op jit(solution)/shard_map/ppermute | solution.py:175
  409.1 13.0 %collective-permute-done.27 = bf16[128,2048]{1,0:T(8,128)(2,1)} collective-permute-done((bf16[128,2048]{1,0:T(8,128)(2,1)S(1)}, bf16[128,2048]{1,0:T(8,128)(2,1)}, u32[]{:S(2)}, u32[]{:S(2)}) %collective-permute-start.27) | collective-permute-done | bytes 524320 | tf_op jit(solution)/shard_map/ppermute | solution.py:175
  438.2 3.7 convolution_convert_fusion.6
  446.7 3.4 fusion.22
  453.1 3.5 multiply_reduce_fusion.1
  460.7 5.6 convolution_convert_fusion
  468.7 4.8 convolution_convert_fusion.5
  477.9 9.0 %collective-permute-done.28 = bf16[128,2048]{1,0:T(8,128)(2,1)S(1)} collective-permute-done((bf16[128,2048]{1,0:T(8,128)(2,1)S(1)}, bf16[128,2048]{1,0:T(8,128)(2,1)S(1)}, u32[]{:S(2)}, u32[]{:S(2)}) %collective-permute-start.28) | collective-permute-done | bytes 524320 | tf_op jit(solution)/shard_map/ppermute | solution.py:175
  486.9 30.2 %collective-permute-done.29 = bf16[128,2048]{1,0:T(8,128)(2,1)S(1)} collective-permute-done((bf16[128,2048]{1,0:T(8,128)(2,1)S(1)}, bf16[128,2048]{1,0:T(8,128)(2,1)S(1)}, u32[]{:S(2)}, u32[]{:S(2)}) %collective-permute-start.29) | collective-permute-done | bytes 524320 | tf_op jit(solution)/shard_map/ppermute | solution.py:175
  518.1 48.7 %psum.7 = f32[4352]{0:T(1024)S(1)} all-reduce(f32[4352]{0:T(1024)S(1)} %pad_maximum_fusion.15), channel_id=1, replica_groups=mesh['fsdp'=8,'tp'=4] {'fsdp','tp'}, use_global_device_ids=true, to_apply=%region_18.19 | all-reduce | flops 4352 | bytes 34816 | tf_op jit(solution)/shard_map/psum | solution.py:330
  (372 shorter events, 157.4 us)
Async XLA Ops:
  7.2 73.1 %all-gather.7.cloned.1.call-start = ((), (), s32[]{:S(2)}) async-start(), calls=%async_computation.5 | async-start | bytes 4718592 | tf_op jit(solution)/shard_map/all_gather | solution.py:212
  9.3 92.6 %all-gather.9.cloned.1.call-start = ((), (), s32[]{:S(2)}) async-start(), calls=%async_computation.6 | async-start | bytes 2359296 | tf_op jit(solution)/shard_map/all_gather | solution.py:215
  10.1 190.9 %all-gather.15.cloned.1.call-start = ((), (), s32[]{:S(2)}) async-start(), calls=%async_computation.9 | async-start | bytes 3932160 | tf_op jit(solution)/shard_map/all_gather | solution.py:233
  14.3 203.3 %all-gather.13.cloned.1.call-start = ((), (), s32[]{:S(2)}) async-start(), calls=%async_computation.8 | async-start | bytes 3932160 | tf_op jit(solution)/shard_map/all_gather | solution.py:233
  14.4 35.1 %collective-permute-start = (bf16[128,2048]{1,0:T(8,128)(2,1)S(1)}, bf16[128,2048]{1,0:T(8,128)(2,1)S(1)}, u32[]{:S(2)}, u32[]{:S(2)}) collective-permute-start(bf16[128,2048]{1,0:T(8,128)(2,1)S(1)} %copy-done.5), channel_id=1, source_target_pairs={{0,1},{1,2},{2,3},{3,0},{4,5},{5,6},{6,7},{7,4},{8,9},{9,10},{10,1... | collective-permute-start | bytes 1572872 | tf_op jit(solution)/shard_map/ppermute | solution.py:175
  18.2 46.2 %collective-permute-start.11 = (bf16[256,768]{1,0:T(8,128)(2,1)}, bf16[256,768]{1,0:T(8,128)(2,1)S(1)}, u32[]{:S(2)}, u32[]{:S(2)}) collective-permute-start(bf16[256,768]{1,0:T(8,128)(2,1)} %get-tuple-element.132), channel_id=1, source_target_pairs={{0,4},{4,0},{8,12},{12,8},{16,20},{20,16},{24,28},{28,24},{1,5},{5... | collective-permute-start | bytes 1179656 | tf_op jit(solution)/shard_map/ppermute | solution.py:172
  18.2 47.4 %collective-permute-start.17 = (bf16[128,2048]{1,0:T(8,128)(2,1)S(1)}, bf16[128,2048]{1,0:T(8,128)(2,1)}, u32[]{:S(2)}, u32[]{:S(2)}) collective-permute-start(bf16[128,2048]{1,0:T(8,128)(2,1)S(1)} %copy-done.26), channel_id=1, source_target_pairs={{0,1},{1,2},{2,3},{3,0},{4,5},{5,6},{6,7},{7,4},{8,9},{9,10},{10,1... | collective-permute-start | bytes 1572872 | tf_op jit(solution)/shard_map/ppermute | solution.py:175
  62.0 16.7 %collective-permute-start.2 = (bf16[128,2048]{1,0:T(8,128)(2,1)S(1)}, bf16[128,2048]{1,0:T(8,128)(2,1)}, u32[]{:S(2)}, u32[]{:S(2)}) collective-permute-start(bf16[128,2048]{1,0:T(8,128)(2,1)S(1)} %collective-permute-done.1), channel_id=1, source_target_pairs={{0,1},{1,2},{2,3},{3,0},{4,5},{5,6},{6,7},{7,4},{8,9},{9,10},{10,1... | collective-permute-start | bytes 1572872 | tf_op jit(solution)/shard_map/ppermute | solution.py:175
  65.6 160.4 %all-gather.11.cloned.1.call-start = ((), (), s32[]{:S(2)}) async-start(), calls=%async_computation.7 | async-start | bytes 3932160 | tf_op jit(solution)/shard_map/all_gather | solution.py:233
  65.6 41.6 %collective-permute-start.18 = (bf16[128,2048]{1,0:T(8,128)(2,1)}, bf16[128,2048]{1,0:T(8,128)(2,1)}, u32[]{:S(2)}, u32[]{:S(2)}) collective-permute-start(bf16[128,2048]{1,0:T(8,128)(2,1)} %collective-permute-done.17), channel_id=1, source_target_pairs={{0,1},{1,2},{2,3},{3,0},{4,5},{5,6},{6,7},{7,4},{8,9},{9,10},{10,1... | collective-permute-start | bytes 1572872 | tf_op jit(solution)/shard_map/ppermute | solution.py:175
  105.2 19.3 %collective-permute-start.3 = (bf16[128,2048]{1,0:T(8,128)(2,1)S(1)}, bf16[128,2048]{1,0:T(8,128)(2,1)S(1)}, u32[]{:S(2)}, u32[]{:S(2)}) collective-permute-start(bf16[128,2048]{1,0:T(8,128)(2,1)S(1)} %get-tuple-element.105), channel_id=1, source_target_pairs={{0,3},{1,0},{2,1},{3,2},{4,7},{5,4},{6,5},{7,6},{8,11},{9,8},{10,9... | collective-permute-start | bytes 1572872 | tf_op jit(solution)/shard_map/ppermute | solution.py:175
  105.2 47.5 %collective-permute-start.4 = (bf16[128,2048]{1,0:T(8,128)(2,1)S(1)}, bf16[128,2048]{1,0:T(8,128)(2,1)S(1)}, u32[]{:S(2)}, u32[]{:S(2)}) collective-permute-start(bf16[128,2048]{1,0:T(8,128)(2,1)S(1)} %get-tuple-element.107), channel_id=1, source_target_pairs={{0,2},{1,3},{2,0},{3,1},{4,6},{5,7},{6,4},{7,5},{8,10},{9,11},{10,... | collective-permute-start | bytes 1572872 | tf_op jit(solution)/shard_map/ppermute | solution.py:175
  105.3 47.5 %collective-permute-start.5 = (bf16[128,2048]{1,0:T(8,128)(2,1)S(1)}, bf16[128,2048]{1,0:T(8,128)(2,1)S(1)}, u32[]{:S(2)}, u32[]{:S(2)}) collective-permute-start(bf16[128,2048]{1,0:T(8,128)(2,1)S(1)} %get-tuple-element.106), channel_id=1, source_target_pairs={{0,1},{1,2},{2,3},{3,0},{4,5},{5,6},{6,7},{7,4},{8,9},{9,10},{10,1... | collective-permute-start | bytes 1572872 | tf_op jit(solution)/shard_map/ppermute | solution.py:175
  107.2 47.8 %collective-permute-start.19 = (bf16[128,2048]{1,0:T(8,128)(2,1)}, bf16[128,2048]{1,0:T(8,128)(2,1)S(1)}, u32[]{:S(2)}, u32[]{:S(2)}) collective-permute-start(bf16[128,2048]{1,0:T(8,128)(2,1)} %collective-permute-done.18), channel_id=1, source_target_pairs={{0,1},{1,2},{2,3},{3,0},{4,5},{5,6},{6,7},{7,4},{8,9},{9,10},{10,1... | collective-permute-start | bytes 1572872 | tf_op jit(solution)/shard_map/ppermute | solution.py:175
  158.0 39.8 %collective-permute-start.20 = (bf16[512,2048]{1,0:T(8,128)(2,1)}, bf16[512,2048]{1,0:T(8,128)(2,1)}, u32[]{:S(2)}, u32[]{:S(2)}) collective-permute-start(bf16[512,2048]{1,0:T(8,128)(2,1)} %pad_maximum_fusion.2), channel_id=1, source_target_pairs={{0,4},{4,0},{8,12},{12,8},{16,20},{20,16},{24,28},{28,24},{1,5},{5... | collective-permute-start | bytes 6291464 | tf_op jit(solution)/shard_map/ppermute | solution.py:172
  168.7 401.1 %reduce-scatter.14.cloned.1.call-start = ((), (), s32[]{:S(2)}) async-start(), calls=%async_computation.14 | async-start | bytes 3932160 | tf_op jit(solution)/shard_map/reduce_scatter | solution.py:309
  195.0 19.4 %collective-permute-start.9 = (bf16[512,2048]{1,0:T(8,128)(2,1)}, bf16[512,2048]{1,0:T(8,128)(2,1)}, u32[]{:S(2)}, u32[]{:S(2)}) collective-permute-start(bf16[512,2048]{1,0:T(8,128)(2,1)} %pad_maximum_fusion.1), channel_id=1, source_target_pairs={{0,4},{4,0},{8,12},{12,8},{16,20},{20,16},{24,28},{28,24},{1,5},{5... | collective-permute-start | bytes 6291464 | tf_op jit(solution)/shard_map/ppermute | solution.py:172
  245.4 326.9 %reduce-scatter.12.cloned.1.call-start = ((), (), s32[]{:S(2)}) async-start(), calls=%async_computation.13 | async-start | bytes 3932160 | tf_op jit(solution)/shard_map/reduce_scatter | solution.py:309
  253.4 320.5 %reduce-scatter.10.cloned.1.call-start = ((), (), s32[]{:S(2)}) async-start(), calls=%async_computation.12 | async-start | bytes 3932160 | tf_op jit(solution)/shard_map/reduce_scatter | solution.py:309
  264.8 17.9 %collective-permute-start.21 = (bf16[512,2048]{1,0:T(8,128)(2,1)}, bf16[512,2048]{1,0:T(8,128)(2,1)}, u32[]{:S(2)}, u32[]{:S(2)}) collective-permute-start(bf16[512,2048]{1,0:T(8,128)(2,1)} %slice.175), channel_id=1, source_target_pairs={{0,4},{4,0},{8,12},{12,8},{16,20},{20,16},{24,28},{28,24},{1,5},{5... | collective-permute-start | bytes 6291464 | tf_op jit(solution)/shard_map/ppermute | solution.py:172
  282.6 296.7 %reduce-scatter.8.cloned.1.call-start = ((), (), s32[]{:S(2)}) async-start(), calls=%async_computation.11 | async-start | bytes 2359296 | tf_op jit(solution)/shard_map/reduce_scatter | solution.py:324
  286.1 15.8 %collective-permute-start.22 = (bf16[128,2048]{1,0:T(8,128)(2,1)S(1)}, bf16[128,2048]{1,0:T(8,128)(2,1)S(1)}, u32[]{:S(2)}, u32[]{:S(2)}) collective-permute-start(bf16[128,2048]{1,0:T(8,128)(2,1)S(1)} %get-tuple-element.99), channel_id=1, source_target_pairs={{0,3},{1,0},{2,1},{3,2},{4,7},{5,4},{6,5},{7,6},{8,11},{9,8},{10,9... | collective-permute-start | bytes 1572872 | tf_op jit(solution)/shard_map/ppermute | solution.py:175
  286.1 46.0 %collective-permute-start.23 = (bf16[128,2048]{1,0:T(8,128)(2,1)S(1)}, bf16[128,2048]{1,0:T(8,128)(2,1)S(1)}, u32[]{:S(2)}, u32[]{:S(2)}) collective-permute-start(bf16[128,2048]{1,0:T(8,128)(2,1)S(1)} %get-tuple-element.101), channel_id=1, source_target_pairs={{0,2},{1,3},{2,0},{3,1},{4,6},{5,7},{6,4},{7,5},{8,10},{9,11},{10,... | collective-permute-start | bytes 1572872 | tf_op jit(solution)/shard_map/ppermute | solution.py:175
  286.2 45.9 %collective-permute-start.24 = (bf16[128,2048]{1,0:T(8,128)(2,1)S(1)}, bf16[128,2048]{1,0:T(8,128)(2,1)S(1)}, u32[]{:S(2)}, u32[]{:S(2)}) collective-permute-start(bf16[128,2048]{1,0:T(8,128)(2,1)S(1)} %get-tuple-element.100), channel_id=1, source_target_pairs={{0,1},{1,2},{2,3},{3,0},{4,5},{5,6},{6,7},{7,4},{8,9},{9,10},{10,1... | collective-permute-start | bytes 1572872 | tf_op jit(solution)/shard_map/ppermute | solution.py:175
  290.8 43.1 %collective-permute-start.14 = (bf16[128,2048]{1,0:T(8,128)(2,1)S(1)}, bf16[128,2048]{1,0:T(8,128)(2,1)S(1)}, u32[]{:S(2)}, u32[]{:S(2)}) collective-permute-start(bf16[128,2048]{1,0:T(8,128)(2,1)S(1)} %get-tuple-element.102), channel_id=1, source_target_pairs={{0,3},{1,0},{2,1},{3,2},{4,7},{5,4},{6,5},{7,6},{8,11},{9,8},{10,9... | collective-permute-start | bytes 1572872 | tf_op jit(solution)/shard_map/ppermute | solution.py:175
  293.1 82.5 %collective-permute-start.15 = (bf16[128,2048]{1,0:T(8,128)(2,1)S(1)}, bf16[128,2048]{1,0:T(8,128)(2,1)S(1)}, u32[]{:S(2)}, u32[]{:S(2)}) collective-permute-start(bf16[128,2048]{1,0:T(8,128)(2,1)S(1)} %get-tuple-element.104), channel_id=1, source_target_pairs={{0,2},{1,3},{2,0},{3,1},{4,6},{5,7},{6,4},{7,5},{8,10},{9,11},{10,... | collective-permute-start | bytes 1572872 | tf_op jit(solution)/shard_map/ppermute | solution.py:175
  301.9 73.8 %collective-permute-start.16 = (bf16[128,2048]{1,0:T(8,128)(2,1)S(1)}, bf16[128,2048]{1,0:T(8,128)(2,1)S(1)}, u32[]{:S(2)}, u32[]{:S(2)}) collective-permute-start(bf16[128,2048]{1,0:T(8,128)(2,1)S(1)} %get-tuple-element.103), channel_id=1, source_target_pairs={{0,1},{1,2},{2,3},{3,0},{4,5},{5,6},{6,7},{7,4},{8,9},{9,10},{10,1... | collective-permute-start | bytes 1572872 | tf_op jit(solution)/shard_map/ppermute | solution.py:175
  378.7 14.8 %collective-permute-start.25 = (bf16[128,2048]{1,0:T(8,128)(2,1)S(1)}, bf16[128,2048]{1,0:T(8,128)(2,1)S(1)}, u32[]{:S(2)}, u32[]{:S(2)}) collective-permute-start(bf16[128,2048]{1,0:T(8,128)(2,1)S(1)} %get-tuple-element.72), channel_id=1, source_target_pairs={{0,1},{1,2},{2,3},{3,0},{4,5},{5,6},{6,7},{7,4},{8,9},{9,10},{10,1... | collective-permute-start | bytes 1572872 | tf_op jit(solution)/shard_map/ppermute | solution.py:175
  393.5 14.7 %collective-permute-start.26 = (bf16[128,2048]{1,0:T(8,128)(2,1)S(1)}, bf16[128,2048]{1,0:T(8,128)(2,1)S(1)}, u32[]{:S(2)}, u32[]{:S(2)}) collective-permute-start(bf16[128,2048]{1,0:T(8,128)(2,1)S(1)} %collective-permute-done.25), channel_id=1, source_target_pairs={{0,1},{1,2},{2,3},{3,0},{4,5},{5,6},{6,7},{7,4},{8,9},{9,10},{10,1... | collective-permute-start | bytes 1572872 | tf_op jit(solution)/shard_map/ppermute | solution.py:175
  442.0 139.1 %reduce-scatter.6.cloned.1.call-start = ((), (), s32[]{:S(2)}) async-start(), calls=%async_computation.10 | async-start | bytes 4718592 | tf_op jit(solution)/shard_map/reduce_scatter | solution.py:327
  474.2 43.0 %collective-permute-start.29 = (bf16[128,2048]{1,0:T(8,128)(2,1)S(1)}, bf16[128,2048]{1,0:T(8,128)(2,1)S(1)}, u32[]{:S(2)}, u32[]{:S(2)}) collective-permute-start(bf16[128,2048]{1,0:T(8,128)(2,1)S(1)} %get-tuple-element.98), channel_id=1, source_target_pairs={{0,2},{1,3},{2,0},{3,1},{4,6},{5,7},{6,4},{7,5},{8,10},{9,11},{10,... | collective-permute-start | bytes 1572872 | tf_op jit(solution)/shard_map/ppermute | solution.py:175
  474.2 43.0 %collective-permute-start.30 = (bf16[128,2048]{1,0:T(8,128)(2,1)S(1)}, bf16[128,2048]{1,0:T(8,128)(2,1)S(1)}, u32[]{:S(2)}, u32[]{:S(2)}) collective-permute-start(bf16[128,2048]{1,0:T(8,128)(2,1)S(1)} %get-tuple-element.97), channel_id=1, source_target_pairs={{0,1},{1,2},{2,3},{3,0},{4,5},{5,6},{6,7},{7,4},{8,9},{9,10},{10,1... | collective-permute-start | bytes 1572872 | tf_op jit(solution)/shard_map/ppermute | solution.py:175
  (95 other events, 982.9 us)
Sparse Core Ops, SparseCore 0:
  10.5 39.5 all-gather.6
  51.9 28.0 all-gather.8
  82.4 43.6 all-gather.14
  128.4 43.8 all-gather.12
  174.6 47.5 all-gather.10
  245.5 49.1 reduce-scatter.13
  297.7 43.9 reduce-scatter.11
  344.6 43.8 reduce-scatter.9
  442.1 46.6 reduce-scatter.7
  492.0 51.2 reduce-scatter.5
